TPU v7x, 256 devices: a whole 4x4x8 slice. The times are simulated.
256 devices in a mesh: dp: 2 (over core), width: 4 (over x), vocab: 32 (over z, y).
Axes of the slice: x: 4, y: 4, z: 8, core: 2. Of those that a mesh axis runs over, the one named last changes fastest.
Arguments:
- hidden: bfloat16 [1024, 8192], P('dp', 'width'), may hold values from -68 to 68
- head: bfloat16 [8192, 2, 32064], P('width', 'dp', 'vocab'), may hold values from -0.25 to 0.25
- teacher: bfloat16 [1024, 2, 32064], P('dp', None, 'vocab'), may hold values from -180 to 180
Outputs:
- divergence: float32 [1024], P('dp')
- grad_head: bfloat16 [8192, 2, 32064], P('width', 'dp', 'vocab')
- grad_hidden: bfloat16 [1024, 8192], P('dp', 'width')
All inputs are finite; a program needn't handle non-finite values.
Results may differ from a plain program's by a relative error of at most 0.0052.
Values may be sent and summed in bfloat16 or wider, within the bound.
A program may use at most 128 MiB of HBM per device.

v0:
```python
import jax
import jax.numpy as jnp
from jax import lax
from jax.sharding import PartitionSpec as P

VOCAB = 64128


def body(hidden, head, teacher):
    tok_rows, width_cols = hidden.shape
    halves = teacher.shape[1]
    local_cols = teacher.shape[2]
    full_head = lax.all_gather(head, "dp", axis=1, tiled=True).reshape(
        width_cols, halves * local_cols
    )
    partial_value = jnp.dot(hidden, full_head, preferred_element_type=jnp.float32)
    student = lax.psum(partial_value, "width")
    target = teacher.reshape(tok_rows, halves * local_cols).astype(jnp.float32)
    student_peak = jnp.max(student, axis=1)
    target_peak = jnp.max(target, axis=1)
    student_peak, target_peak = lax.pmax((student_peak, target_peak), "vocab")
    target_exp = jnp.exp(target - target_peak[:, None])
    student_total, target_total, cross_total = lax.psum(
        (
            jnp.sum(jnp.exp(student - student_peak[:, None]), axis=1),
            jnp.sum(target_exp, axis=1),
            jnp.sum(target_exp * (target - student), axis=1),
        ),
        "vocab",
    )
    student_lse = student_peak + jnp.log(student_total)
    target_lse = target_peak + jnp.log(target_total)
    divergence = cross_total / target_total - target_lse + student_lse
    prob_student = jnp.exp(student - student_lse[:, None])
    prob_target = jnp.exp(target - target_lse[:, None])
    grad = (VOCAB * (prob_student - prob_target)).astype(jnp.bfloat16)
    grad_blocks = grad.reshape(tok_rows, halves, local_cols)
    blocks = width_cols * lax.axis_size("dp") // width_cols
    term = jnp.einsum("td,tkv->kdv", hidden, grad_blocks, preferred_element_type=jnp.float32)
    head_term = lax.psum_scatter(
        term.reshape(blocks * width_cols, local_cols), "dp", scatter_dimension=0, tiled=True
    )
    grad_head = head_term.astype(jnp.bfloat16).reshape(width_cols, 1, local_cols)
    hidden_term = lax.dot_general(
        grad, full_head, (((1,), (1,)), ((), ())), preferred_element_type=jnp.float32
    )
    grad_hidden = lax.psum(hidden_term, "vocab").astype(jnp.bfloat16)
    return (divergence, grad_head, grad_hidden)


def solution(mesh):
    return jax.shard_map(
        body,
        mesh=mesh,
        in_specs=(P("dp", "width"), P("width", "dp", "vocab"), P("dp", None, "vocab")),
        out_specs=(P("dp"), P("width", "dp", "vocab"), P("dp", "width")),
        check_vma=False,
    )
```

profile of v0, /device:TPU:2, one launch (start us, length us, event | category | flops | bytes accessed | tf_op | source)
XLA Modules:
  0.0 548.4 jit_solution(12567613389792812008)
XLA Ops:
  7.2 0.0 copy-start
  7.2 0.0 all-gather.2.cloned.1.call-start
  7.2 0.7 all-gather.2.cloned.1.call-update
  7.9 0.0 all-reduce.6.cloned.1.call-start
  8.0 29.8 %all-gather.2.cloned.1.call-done = bf16[2048,2,1002]{0,2,1:T(8,128)(2,1)} async-done(((bf16[2048,1,1002]{0,2,1:T(8,128)(2,1)}), bf16[2048,2,1002]{0,2,1:T(8,128)(2,1)}) %all-gather.2.cloned.1.call-update) | async-done | bytes 8208400 | tf_op jit(solution)/shard_map/all_gather | solution.py:13
  37.8 8.1 %reshape.29 = bf16[2048,2004]{0,1:T(8,128)(2,1)} reshape(bf16[2048,2,1002]{0,2,1:T(8,128)(2,1)} %all-gather.2.cloned.1.call-done) | data formatting | bytes 16416768 | tf_op jit(solution)/shard_map/reshape | solution.py:13
  45.9 0.0 copy-done
  45.9 8.8 %fusion.1 = f32[512,2004]{0,1:T(8,128)} fusion(bf16[512,2048]{1,0:T(8,128)(2,1)S(1)} %copy-done, bf16[2048,2004]{0,1:T(8,128)(2,1)} %reshape.29), kind=kOutput, calls=%fused_computation.10 | convolution fusion | flops 4202692608 | bytes 14409728 | tf_op jit(solution)/shard_map/dot_general | solution.py:16
  54.7 0.0 all-reduce.6.cloned.1.call-update
  54.7 0.0 reduce-scatter.2.cloned.1.call-start
  54.7 4.2 copy.13
  58.9 3.3 reduce_max.23
  62.2 4.5 reshape.33
  66.7 84.9 %all-reduce.6.cloned.1.call-done = f32[512,2004]{0,1:T(8,128)} async-done(((f32[512,2004]{0,1:T(8,128)}), f32[512,2004]{0,1:T(8,128)}) %all-reduce.6.cloned.1.call-update) | async-done | bytes 4104208 | tf_op jit(solution)/shard_map/psum | solution.py:17
  151.7 2.5 reduce_max.25
  154.2 75.3 %all-reduce.2 = (f32[512]{0:T(512)S(1)}, f32[512]{0:T(512)S(1)}) all-reduce(f32[512]{0:T(512)S(1)} %reduce_max.25, bf16[512]{0:T(512)(128)(2,1)S(1)} %reduce_max.23), channel_id=1, replica_groups=mesh['dp'=2,'width'=4,'vocab'=32] {'vocab'}, use_global_device_ids=true, to_apply=%region_8.0 | all-reduce | flops 1024 | bytes 7168 | tf_op jit(solution)/shard_map/pmax | solution.py:21
  229.4 4.9 exponential_reduce_fusion.1
  234.3 4.8 multiply_reduce_fusion
  239.1 69.6 %all-reduce.1 = (f32[512]{0:T(512)S(1)}, f32[512]{0:T(512)S(1)}) all-reduce(f32[512]{0:T(512)S(1)} %get-tuple-element.13, f32[512]{0:T(512)S(1)} %exponential_reduce_fusion.1), channel_id=1, replica_groups=mesh['dp'=2,'width'=4,'vocab'=32] {'vocab'}, use_global_device_ids=true, to_apply=%region_10.0 | all-reduce | flops 1024 | bytes 8192 | tf_op jit(solution)/shard_map/psum | solution.py:23
  308.7 5.9 %multiply_convert_fusion = bf16[512,2004]{0,1:T(8,128)(2,1)} fusion(f32[512,2004]{0,1:T(8,128)} %reshape.33, f32[512,2004]{0,1:T(8,128)} %all-reduce.6.cloned.1.call-done, f32[512]{0:T(512)S(1)} %get-tuple-element.21, f32[512]{0:T(512)S(1)} %get-tuple-element.20), kind=kLoop, calls=%fused_computation.2 | loop fusion | flops 5130240 | bytes 10264576 | tf_op jit(solution)/shard_map/convert_element_type | solution.py:36
  314.6 3.3 reshape.30
  317.9 9.5 %convolution_bitcast_fusion = f32[2,2048,1002]{1,2,0:T(8,128)} fusion(bf16[512,2,1002]{0,2,1:T(8,128)(2,1)} %reshape.30, bf16[512,2048]{1,0:T(8,128)(2,1)S(1)} %copy-done), kind=kOutput, calls=%fused_computation | convolution fusion | flops 4202692608 | bytes 20566016 | tf_op jit(solution)/shard_map/td,tkv->kdv/dot_general | solution.py:39
  327.4 17.9 %copy.14 = f32[2,2048,1002]{2,1,0:T(8,128)} copy(f32[2,2048,1002]{1,2,0:T(8,128)} %convolution_bitcast_fusion) | data formatting | bytes 32833536 | tf_op jit(solution)/shard_map/td,tkv->kdv/transpose | solution.py:39
  345.3 0.0 copy-start.2
  345.3 0.0 reduce-scatter.2.cloned.1.call-update
  345.4 1.6 copy-done.2
  346.9 9.5 %fusion.2 = f32[512,2048]{1,0:T(8,128)} fusion(bf16[512,2004]{0,1:T(8,128)(2,1)S(1)} %copy-done.2, bf16[2048,2004]{0,1:T(8,128)(2,1)} %reshape.29), kind=kOutput, calls=%fused_computation.11 | convolution fusion | flops 4202692608 | bytes 14454784 | tf_op jit(solution)/shard_map/dot_general | solution.py:44
  356.4 172.3 %all-reduce.7 = (f32[512]{0:T(512)S(1)}, bf16[512,2048]{1,0:T(8,128)(2,1)}) all-reduce(f32[512]{0:T(512)S(1)} %get-tuple-element.12, f32[512,2048]{1,0:T(8,128)} %fusion.2), channel_id=1, replica_groups=mesh['dp'=2,'width'=4,'vocab'=32] {'vocab'}, use_global_device_ids=true, to_apply=%region_4.0 | all-reduce | flops 1049088 | bytes 6295552 | tf_op jit(solution)/shard_map/psum | solution.py:23
  528.7 0.6 subtract_add_fusion
  529.3 0.0 reduce-scatter.2.cloned.1.call-done
  529.3 0.0 copy-start.1
  529.3 6.1 %convert_bitcast_fusion = bf16[2048,1,1002]{2,0,1:T(8,128)(2,1)} fusion(f32[2048,1002]{1,0:T(8,128)} %reduce-scatter.2.cloned.1.call-done), kind=kLoop, calls=%fused_computation.1 | loop fusion | flops 2052096 | bytes 12312576 | tf_op jit(solution)/shard_map/reshape | solution.py:43
  535.4 6.5 %copy.15 = bf16[2048,1,1002]{0,2,1:T(8,128)(2,1)} copy(bf16[2048,1,1002]{2,0,1:T(8,128)(2,1)} %convert_bitcast_fusion) | data formatting | bytes 8208384
  541.9 0.0 copy-done.1
  (1 shorter events, 0.0 us)
Async XLA Ops:
  7.2 38.7 %copy-start = (bf16[512,2048]{1,0:T(8,128)(2,1)S(1)}, bf16[512,2048]{1,0:T(8,128)(2,1)}, u32[]{:S(2)}) copy-start(bf16[512,2048]{1,0:T(8,128)(2,1)} %param.3) | copy-start | bytes 6291460
  7.2 30.6 %all-gather.2.cloned.1.call-start = ((), (), s32[]{:S(2)}) async-start(), calls=%async_computation.1 | async-start | bytes 12386304 | tf_op jit(solution)/shard_map/all_gather | solution.py:13
  7.9 143.7 %all-reduce.6.cloned.1.call-start = ((), (), s32[]{:S(2)}) async-start(), calls=%async_computation.2 | async-start | bytes 8224768 | tf_op jit(solution)/shard_map/psum | solution.py:17
  54.7 474.6 %reduce-scatter.2.cloned.1.call-start = ((), (), s32[]{:S(2)}) async-start(), calls=%async_computation.3 | async-start | bytes 25165824 | tf_op jit(solution)/shard_map/reduce_scatter | solution.py:40
  345.3 1.6 copy-start.2
  529.3 12.6 %copy-start.1 = (bf16[512,2048]{1,0:T(8,128)(2,1)S(1)}, bf16[512,2048]{1,0:T(8,128)(2,1)}, u32[]{:S(2)}) copy-start(bf16[512,2048]{1,0:T(8,128)(2,1)} %param.3) | copy-start | bytes 6291460
Sparse Core Ops, SparseCore 0:
  9.8 27.9 all-gather.1
  54.8 96.8 all-reduce.5
  345.5 27.6 reduce-scatter.1
where the time goes:
time: 549 us; the launch traced here: 548 us
  blocking collectives  317 us (58%)
  waiting for transfers between devices  115 us (21%)
  local copies, waits for them, and re-layouts  46 us (8%)
  other arithmetic  28.1 us (5%)
  matrix products  27.7 us (5%)
  between operations  13.8 us (3%)
    psum x2, blocking collectives, body(): lax.psum((jnp.sum(jnp.exp(student - student_peak[:, None]), axis=1), jnp....  242 us
    psum x1, waiting for transfers between devices, body(): student = lax.psum(partial_value, 'width')  84.9 us
    pmax x1, blocking collectives, body(): student_peak, target_peak = lax.pmax((student_peak, target_peak), 'vocab')  75.3 us
    all_gather x1, waiting for transfers between devices, body(): lax.all_gather(head, 'dp', axis=1, tiled=True)  29.8 us
    transpose x1, local copies, waits for them, and re-layouts, body(): jnp.einsum('td,tkv->kdv', hidden, grad_blocks, preferred_element_type=jnp...  17.9 us
  transfers between devices with their start and end apart: 3, of which 2 were waited for; matrix products, arithmetic and copies ran while one was open for 4% of the time, Pallas kernels for 0%

commit v1 on v0

--- a/solution.py
+++ b/solution.py
@@ -14,7 +14,7 @@
         width_cols, halves * local_cols
     )
     partial_value = jnp.dot(hidden, full_head, preferred_element_type=jnp.float32)
-    student = lax.psum(partial_value, "width")
+    student = jnp.sum(lax.all_gather(partial_value, "width"), axis=0)
     target = teacher.reshape(tok_rows, halves * local_cols).astype(jnp.float32)
     student_peak = jnp.max(student, axis=1)
     target_peak = jnp.max(target, axis=1)

time: 549 us -> 649 us (1.18)
  waiting for transfers between devices: 115 us -> 182 us
  other arithmetic: 28.1 us -> 43.5 us
  local copies, waits for them, and re-layouts: 46 us -> 58.7 us
    all_gather x0 -> x1, waiting for transfers between devices: none -> 152 us  [body(): student = jnp.sum(lax.all_gather(partial_value, 'width'), axis=0)]
    psum x1 -> x0, waiting for transfers between devices: 84.9 us -> none  [body(): student = lax.psum(partial_value, 'width')]
    reduce_sum x1 -> x2, other arithmetic: 4.76 us -> 27.7 us  [the longest x1 24.8 us: body(): student = jnp.sum(lax.all_gather(partial_value, 'width'), axis=0)]
    all_gather x0 -> x1, local copies, waits for them, and re-layouts: none -> 20.1 us  [body(): student = jnp.sum(lax.all_gather(partial_value, 'width'), axis=0)]
    convert_element_type x2 -> x0, local copies, waits for them, and re-layouts: 8.68 us -> none  [body(): target = teacher.reshape(tok_rows, halves * local_cols).astype(jnp.float32)]
  transfers between devices with their start and end apart: 3 -> 3, of which waited for: 2 -> 2; matrix products, arithmetic and copies ran while one was open for 4% -> 2% of each run, Pallas kernels for 0% -> 0%
where the time goes in v1:
time: 649 us; the launch traced here: 647 us
  blocking collectives  317 us (49%)
  waiting for transfers between devices  182 us (28%)
  local copies, waits for them, and re-layouts  58.7 us (9%)
  other arithmetic  43.5 us (7%)
  matrix products  32.3 us (5%)
  between operations  13.8 us (2%)
    psum x2, blocking collectives, body(): lax.psum((jnp.sum(jnp.exp(student - student_peak[:, None]), axis=1), jnp....  241 us
    all_gather x1, waiting for transfers between devices, body(): student = jnp.sum(lax.all_gather(partial_value, 'width'), axis=0)  152 us
    pmax x1, blocking collectives, body(): student_peak, target_peak = lax.pmax((student_peak, target_peak), 'vocab')  75.3 us
    all_gather x1, waiting for transfers between devices, body(): lax.all_gather(head, 'dp', axis=1, tiled=True)  29.8 us
    reduce_sum x1, other arithmetic, body(): student = jnp.sum(lax.all_gather(partial_value, 'width'), axis=0)  24.8 us
    all_gather x1, local copies, waits for them, and re-layouts, body(): student = jnp.sum(lax.all_gather(partial_value, 'width'), axis=0)  20.1 us
    transpose x1, local copies, waits for them, and re-layouts, body(): jnp.einsum('td,tkv->kdv', hidden, grad_blocks, preferred_element_type=jnp...  17.9 us
  transfers between devices with their start and end apart: 3, of which 2 were waited for; matrix products, arithmetic and copies ran while one was open for 2% of the time, Pallas kernels for 0%

profile of v1, /device:TPU:2, one launch (start us, length us, event | category | flops | bytes accessed | tf_op | source)
XLA Modules:
  0.0 647.4 jit_solution(9629284523927074222)
XLA Ops:
  7.2 0.0 copy-start
  7.2 0.0 all-gather.4.cloned.1.call-start
  7.2 0.7 all-gather.4.cloned.1.call-update
  7.9 0.0 all-gather.6.cloned.1.call-start
  8.0 29.8 %all-gather.4.cloned.1.call-done = bf16[2048,2,1002]{0,2,1:T(8,128)(2,1)} async-done(((bf16[2048,1,1002]{0,2,1:T(8,128)(2,1)}), bf16[2048,2,1002]{0,2,1:T(8,128)(2,1)}) %all-gather.4.cloned.1.call-update) | async-done | bytes 8208400 | tf_op jit(solution)/shard_map/all_gather | solution.py:13
  37.8 8.1 %reshape.52 = bf16[2048,2004]{0,1:T(8,128)(2,1)} reshape(bf16[2048,2,1002]{0,2,1:T(8,128)(2,1)} %all-gather.4.cloned.1.call-done) | data formatting | bytes 16416768 | tf_op jit(solution)/shard_map/reshape | solution.py:13
  45.9 0.0 copy-done
  45.9 8.9 %fusion.11 = f32[512,2004]{0,1:T(8,128)} fusion(bf16[512,2048]{1,0:T(8,128)(2,1)S(1)} %copy-done, bf16[2048,2004]{0,1:T(8,128)(2,1)} %reshape.52), kind=kOutput, calls=%fused_computation.19 | convolution fusion | flops 4202692608 | bytes 14409728 | tf_op jit(solution)/shard_map/dot_general | solution.py:16
  54.7 0.0 all-gather.6.cloned.1.call-update
  54.7 0.0 reduce-scatter.2.cloned.1.call-start
  54.8 3.3 reduce_max.23
  58.1 151.9 %all-gather.6.cloned.1.call-done = f32[2048,2004]{0,1:T(8,128)} async-done(((f32[512,2004]{0,1:T(8,128)}), f32[2048,2004]{0,1:T(8,128)}) %all-gather.6.cloned.1.call-update) | async-done | bytes 16416784 | tf_op jit(solution)/shard_map/all_gather | solution.py:17
  210.0 20.1 %reshape.55 = f32[4,512,2004]{1,0,2:T(4,128)} reshape(f32[2048,2004]{0,1:T(8,128)} %all-gather.6.cloned.1.call-done) | data formatting | bytes 32833536 | tf_op jit(solution)/shard_map/all_gather | solution.py:17
  230.1 24.8 %reduce_sum.38 = f32[512,2004]{0,1:T(8,128)} reduce(f32[4,512,2004]{1,0,2:T(4,128)} %reshape.55, f32[]{:T(128)} %constant.2.clone.1), dimensions={0}, to_apply=%region_2.0 | reduce | flops 3078144 | bytes 20520964 | tf_op jit(solution)/shard_map/reduce_sum | solution.py:17
  254.9 4.5 reduce_sum.39
  259.4 2.5 reduce_max.25
  261.9 75.3 %all-reduce.2 = (f32[512]{0:T(512)S(1)}, f32[512]{0:T(512)S(1)}) all-reduce(f32[512]{0:T(512)S(1)} %reduce_max.25, bf16[512]{0:T(512)(128)(2,1)S(1)} %reduce_max.23), channel_id=1, replica_groups=mesh['dp'=2,'width'=4,'vocab'=32] {'vocab'}, use_global_device_ids=true, to_apply=%region_8.0 | all-reduce | flops 1024 | bytes 7168 | tf_op jit(solution)/shard_map/pmax | solution.py:21
  337.2 0.0 copy-start.2
  337.2 2.9 exponential_reduce_fusion
  340.1 0.0 copy-done.2
  340.1 3.3 fusion.1
  343.4 69.7 %all-reduce.1 = (f32[512]{0:T(512)S(1)}, f32[512]{0:T(512)S(1)}) all-reduce(f32[512]{0:T(512)S(1)} %exponential_reduce_fusion, f32[512]{0:T(512)S(1)} %get-tuple-element.9), channel_id=1, replica_groups=mesh['dp'=2,'width'=4,'vocab'=32] {'vocab'}, use_global_device_ids=true, to_apply=%region_10.0 | all-reduce | flops 1024 | bytes 8192 | tf_op jit(solution)/shard_map/psum | solution.py:23
  413.1 11.3 %convolution_bitcast_fusion = f32[2,2048,1002]{1,2,0:T(8,128)} fusion(bf16[512,2048]{1,0:T(8,128)(2,1)S(1)} %copy-done, f32[512,2,1002]{0,2,1:T(8,128)} %reduce_sum.39, f32[512]{0:T(512)S(1)} %get-tuple-element.18, f32[512]{0:T(512)S(1)} %get-tuple-element.17, bf16[512,2,1002]{0,1,2:T(2,128)(2,1)} %param.5), kind=kOutput, calls=%fused_computation | convolution fusion | flops 4208848896 | bytes 24674304 | tf_op jit(solution)/shard_map/td,tkv->kdv/dot_general | solution.py:39
  424.4 17.9 %copy.12 = f32[2,2048,1002]{2,1,0:T(8,128)} copy(f32[2,2048,1002]{1,2,0:T(8,128)} %convolution_bitcast_fusion) | data formatting | bytes 32833536 | tf_op jit(solution)/shard_map/td,tkv->kdv/transpose | solution.py:39
  442.3 0.0 copy-start.3
  442.3 0.0 reduce-scatter.2.cloned.1.call-update
  442.3 1.5 copy-done.3
  443.9 12.2 %convolution_bitcast_fusion.1 = f32[512,2048]{1,0:T(8,128)} fusion(bf16[2048,2,1002]{0,2,1:T(8,128)(2,1)} %all-gather.4.cloned.1.call-done, f32[512,2,1002]{0,2,1:T(8,128)} %reduce_sum.39, f32[512]{0:T(512)S(1)} %get-tuple-element.18, f32[512]{0:T(512)S(1)} %get-tuple-element.17, bf16[512,2,1002]{0,1,2:T(2,128)(2,1)S(1)} %copy-done.3), kind=kOutput, calls=%fused_computation.14 | convolution fusion | flops 4208848896 | bytes 18563072 | tf_op jit(solution)/shard_map/dot_general | solution.py:44
  456.0 171.7 %all-reduce.4 = (f32[512]{0:T(512)S(1)}, bf16[512,2048]{1,0:T(8,128)(2,1)}) all-reduce(f32[512]{0:T(512)S(1)} %get-tuple-element.10, f32[512,2048]{1,0:T(8,128)} %convolution_bitcast_fusion.1), channel_id=1, replica_groups=mesh['dp'=2,'width'=4,'vocab'=32] {'vocab'}, use_global_device_ids=true, to_apply=%region_4.0 | all-reduce | flops 1049088 | bytes 6295552 | tf_op jit(solution)/shard_map/psum | solution.py:23
  627.7 0.6 subtract_add_fusion
  628.3 0.0 reduce-scatter.2.cloned.1.call-done
  628.3 0.0 copy-start.1
  628.3 6.1 convert_bitcast_fusion
  634.4 6.5 copy.13
  640.9 0.0 copy-done.1
  (1 shorter events, 0.0 us)
Async XLA Ops:
  7.2 38.7 %copy-start = (bf16[512,2048]{1,0:T(8,128)(2,1)S(1)}, bf16[512,2048]{1,0:T(8,128)(2,1)}, u32[]{:S(2)}) copy-start(bf16[512,2048]{1,0:T(8,128)(2,1)} %param.3) | copy-start | bytes 6291460
  7.2 30.6 %all-gather.4.cloned.1.call-start = ((), (), s32[]{:S(2)}) async-start(), calls=%async_computation.1 | async-start | bytes 12386304 | tf_op jit(solution)/shard_map/all_gather | solution.py:13
  7.9 202.1 %all-gather.6.cloned.1.call-start = ((), (), s32[]{:S(2)}) async-start(), calls=%async_computation.3 | async-start | bytes 20561920 | tf_op jit(solution)/shard_map/all_gather | solution.py:17
  54.7 573.6 %reduce-scatter.2.cloned.1.call-start = ((), (), s32[]{:S(2)}) async-start(), calls=%async_computation.2 | async-start | bytes 25165824 | tf_op jit(solution)/shard_map/reduce_scatter | solution.py:40
  337.2 2.9 copy-start.2
  442.3 1.6 copy-start.3
  628.3 12.6 %copy-start.1 = (bf16[512,2048]{1,0:T(8,128)(2,1)S(1)}, bf16[512,2048]{1,0:T(8,128)(2,1)}, u32[]{:S(2)}) copy-start(bf16[512,2048]{1,0:T(8,128)(2,1)} %param.3) | copy-start | bytes 6291460
Sparse Core Ops, SparseCore 0:
  9.8 27.9 all-gather.3
  54.8 155.0 all-gather.5
  442.4 27.6 reduce-scatter.1
